TPU v7x, 256 devices: a whole 4x4x8 slice. The times are simulated.
256 devices in a mesh: seq: 16 (over z, x_lo), wr: 4 (over y), wc: 4 (over x_hi, core).
Axes of the slice: x: 4 (x_hi: 2, x_lo: 2; x = x_hi * 2 + x_lo), y: 4, z: 8, core: 2. Of those that a mesh axis runs over, the one named last changes fastest.
Arguments:
- tokens: bfloat16 [8192, 2048], P('seq', ('wr', 'wc')), may hold values from -6 to 6
- ln_gain: float32 [2, 2048], replicated, may hold values from 0.5 to 1.5
- w_branch: bfloat16 [2, 2048, 4096], P(None, None, ('wr', 'wc')), may hold values from -0.125 to 0.125
- w_outgate: bfloat16 [2, 2048, 4096], P(None, None, ('wr', 'wc')), may hold values from -0.125 to 0.125
- w_gates: bfloat16 [2, 2048, 8], replicated, may hold values from -0.125 to 0.125
- forget_bias: float32 [2, 4], replicated, may hold values from 3.2 to 11
- conv_weight: float32 [2, 4, 4096], P(None, None, ('wr', 'wc')), may hold values from -3 to 3
- conv_bias: float32 [2, 4096], P(None, ('wr', 'wc')), may hold values from -3 to 3
- w_query: float32 [2, 4, 4, 4, 256], P(None, 'wr'), may hold values from -3 to 3
- w_key: float32 [2, 4, 4, 4, 256], P(None, 'wr'), may hold values from -3 to 3
- w_value: float32 [2, 4, 4, 4, 256], P(None, 'wr', None, 'wc'), may hold values from -4 to 4
- skip_gain: float32 [2, 4096], P(None, ('wr', 'wc')), may hold values from 0.5 to 1.5
- norm_gain: float32 [2, 4096], P(None, ('wr', 'wc')), may hold values from 0.5 to 1.5
- w_down: bfloat16 [2, 4096, 2048], P(None, ('wr', 'wc')), may hold values from -0.125 to 0.125
- lengths: int32 [3], replicated, may hold values from 1 to 4096, 8192 in all
- request_prompt: int32 [32], P('seq'), may hold values from 0 to 2
Outputs:
- mixed: bfloat16 [8192, 2048], P('seq', ('wr', 'wc'))
- request_state: bfloat16 [2, 32, 4, 1024, 1024], P(None, 'seq', 'wr', None, 'wc')
- request_conv: bfloat16 [2, 32, 3, 4096], P(None, 'seq', None, ('wr', 'wc'))
Inputs may be any that keep to these rules, and one draw needn't show every extreme that they name: `lengths`: the 3 prompts lie end to end in order and fill all 8192 positions; the longest has exactly 4096 positions.
All inputs are finite; a program needn't handle non-finite values.
Results may differ from a plain program's by a relative error of at most 0.035.
Values may be sent and summed in bfloat16 or wider, within the bound.
A program may use at most 128 MiB of HBM per device.

v0:
```python
import jax
import jax.numpy as jnp
from jax import lax
from jax.sharding import PartitionSpec as P

HEADS = 4
CONV = 4
LAYERS = 2
PROMPTS = 3
EPSILON = 1e-05
GATE_CAP = 15.0
ROW_DIMS = (((0,), (0,)), ((), ()))
FEATURE_DIMS = (((1,), (1,)), ((), ()))


def shifted(value, axis, steps):
    count = lax.axis_size(axis)
    first, last = (max(0, -steps), min(count, count - steps))
    return lax.ppermute(value, axis, [(source, source + steps) for source in range(first, last)])


def span_weights(gathered, lengths, rows, count):
    spans = jnp.arange(count, dtype=jnp.int32)
    seg_end = segment_of(spans * rows + (rows - 1), lengths)
    totals = gathered[:, 0]
    later = jnp.arange(count + 1, dtype=jnp.int32)
    between = (spans[None, None, :] > spans[None, :, None]) & (
        spans[None, None, :] < later[:, None, None]
    )
    logs = jnp.sum(jnp.where(between, totals[None, None, :], 0.0), axis=2)
    seg_in = segment_of(later * rows - 1, lengths)
    keep = (spans[None, :] < later[:, None]) & (seg_end[None, :] == seg_in[:, None])
    state_rows = jnp.where(keep, jnp.exp(logs), 0.0)
    end_rows = []
    for prompt, end_pos in enumerate((lengths[0] - 1, lengths[0] + lengths[1] - 1)):
        holder = end_pos // rows
        pick = (spans == holder).astype(jnp.float32)
        end_cum = jnp.sum(pick * gathered[:, 1 + prompt])
        row = jnp.sum(pick[:, None] * logs[:count], axis=0) + end_cum
        kept = (spans < holder) & (seg_end == prompt)
        kept = kept & (segment_of(holder * rows - 1, lengths) == prompt)
        end_rows.append(jnp.where(kept, jnp.exp(row), 0.0))
    return (state_rows[:count], jnp.stack(end_rows + [state_rows[count]]))


def mix_spans(weights, spans):
    return jnp.sum(weights[:, :, None, None] * spans[None], axis=1)


def norm_rows(source, gain_row):
    widened = source.astype(jnp.float32)
    row_mean = jnp.mean(widened, axis=1, keepdims=True)
    row_var = jnp.mean(widened * widened, axis=1, keepdims=True) - row_mean * row_mean
    return ((widened - row_mean) * lax.rsqrt(row_var + EPSILON) * gain_row).astype(jnp.bfloat16)


def segment_of(positions, lengths):
    bound_one = lengths[0]
    bound_two = lengths[0] + lengths[1]
    return (positions >= bound_one).astype(jnp.int32) + (positions >= bound_two).astype(jnp.int32)


def conv_rows(extended, ext_segment, segment, weight, bias_row):
    row_count = segment.shape[0]
    widened = extended.astype(jnp.float32)
    summed = jnp.zeros((row_count, widened.shape[1]), jnp.float32) + bias_row
    for back_step in range(weight.shape[0]):
        low_row = weight.shape[0] - 1 - back_step
        keep_row = (ext_segment[low_row : low_row + row_count] == segment).astype(jnp.float32)
        summed = (
            summed + weight[back_step] * widened[low_row : low_row + row_count] * keep_row[:, None]
        )
    return jax.nn.silu(summed).astype(jnp.bfloat16)


def block_mix(source, weight):
    row_count = source.shape[0]
    grouped = source.astype(jnp.float32).reshape(row_count, 4, -1)
    mixed = jnp.einsum("tig,ijg->tjg", grouped, weight, precision=lax.Precision.HIGHEST)
    return mixed.reshape(row_count, -1)


def block_terms(queries, key_rows, values, log_forget, in_gate, segment, prev_seg):
    row_count = queries.shape[0]
    cum_log = jnp.cumsum(log_forget)
    row_order = jnp.arange(row_count)
    allowed = (row_order[:, None] >= row_order[None, :]) & (segment[:, None] == segment[None, :])
    exponent = jnp.where(allowed, cum_log[:, None] - cum_log[None, :] + in_gate[None, :], -jnp.inf)
    scores = lax.dot_general(
        queries, key_rows, FEATURE_DIMS, preferred_element_type=jnp.float32
    ) * jnp.exp(exponent)
    in_block = jnp.dot(scores.astype(jnp.bfloat16), values, preferred_element_type=jnp.float32)
    carried = jnp.where(segment == prev_seg, jnp.exp(cum_log), 0.0)
    last_seg = segment[row_count - 1]
    weights = jnp.where(
        segment == last_seg, jnp.exp(cum_log[row_count - 1] - cum_log + in_gate), 0.0
    )
    weighted = (key_rows.astype(jnp.float32) * weights[:, None]).astype(jnp.bfloat16)
    increment = lax.dot_general(weighted, values, ROW_DIMS, preferred_element_type=jnp.float32)
    return (in_block, carried, increment)


def end_part(key_rows, values, cum_log, in_gate, segment, local_end, prompt, holder):
    row_order = jnp.arange(segment.shape[0])
    chosen = holder & (segment == prompt) & (row_order <= local_end)
    weights = jnp.where(chosen, jnp.exp(cum_log[local_end] - cum_log + in_gate), 0.0)
    weighted = (key_rows.astype(jnp.float32) * weights[:, None]).astype(jnp.bfloat16)
    return lax.dot_general(weighted, values, ROW_DIMS, preferred_element_type=jnp.float32)


def body(
    tokens,
    ln_gain,
    w_branch,
    w_outgate,
    w_gates,
    forget_bias,
    conv_weight,
    conv_bias,
    w_query,
    w_key,
    w_value,
    skip_gain,
    norm_gain,
    w_down,
    lengths,
    request_prompt,
):
    tok_rows = tokens.shape[0]
    seq_count = lax.axis_size("seq")
    seq_index = lax.axis_index("seq")
    head_idx = lax.axis_index("wr")
    row_offset = seq_index * tok_rows
    total_rows = tok_rows * seq_count
    row_ids = jnp.arange(tok_rows, dtype=jnp.int32)
    positions = row_offset + row_ids
    segment = segment_of(positions, lengths)
    seg_before = jnp.where(row_offset > 0, segment_of(row_offset - 1, lengths), -1)
    rim_positions = row_offset - (CONV - 1) + jnp.arange(CONV - 1, dtype=jnp.int32)
    rim_segment = jnp.where(rim_positions >= 0, segment_of(rim_positions, lengths), -1)
    ext_segment = jnp.concatenate([rim_segment, segment])
    prompt_starts = [jnp.zeros((), jnp.int32), lengths[0], lengths[0] + lengths[1]]
    prompt_ends = [
        lengths[0] - 1,
        lengths[0] + lengths[1] - 1,
        jnp.zeros((), jnp.int32) + (total_rows - 1),
    ]
    head_mask = (jnp.arange(HEADS, dtype=jnp.int32) == head_idx).astype(jnp.float32)
    current = tokens
    sent_states = []
    sent_edges = []
    for layer_idx in range(LAYERS):
        gathered = lax.all_gather(current, ("wr", "wc"), axis=1, tiled=True)
        normed = norm_rows(gathered, ln_gain[layer_idx])
        branch = jnp.dot(normed, w_branch[layer_idx], preferred_element_type=jnp.float32).astype(
            jnp.bfloat16
        )
        outgate = jnp.dot(normed, w_outgate[layer_idx], preferred_element_type=jnp.float32)
        gate_pre = jnp.dot(normed, w_gates[layer_idx], preferred_element_type=jnp.float32)
        input_pre = jnp.sum(gate_pre[:, :HEADS] * head_mask, axis=1)
        forget_pre = jnp.sum((gate_pre[:, HEADS:] + forget_bias[layer_idx]) * head_mask, axis=1)
        in_gate = GATE_CAP * jnp.tanh(input_pre / GATE_CAP)
        log_forget = jax.nn.log_sigmoid(forget_pre)
        edge_in = shifted(branch[tok_rows - (CONV - 1) :], "seq", 1)
        extended = jnp.concatenate([edge_in, branch], axis=0)
        conv_act = conv_rows(
            extended, ext_segment, segment, conv_weight[layer_idx], conv_bias[layer_idx]
        )
        head_branch, head_act = (
            lax.all_gather(branch, "wc", axis=1, tiled=True),
            lax.all_gather(conv_act, "wc", axis=1, tiled=True),
        )
        head_width = head_act.shape[1]
        queries = block_mix(head_act, w_query[layer_idx, 0]).astype(jnp.bfloat16)
        key_rows = (block_mix(head_act, w_key[layer_idx, 0]) * head_width ** (-0.5)).astype(
            jnp.bfloat16
        )
        values = block_mix(head_branch, w_value[layer_idx, 0]).astype(jnp.bfloat16)
        cum_log = jnp.cumsum(log_forget)
        holders = [
            (end_pos >= row_offset) & (end_pos < row_offset + tok_rows) for end_pos in prompt_ends
        ]
        local_ends = [jnp.clip(end_pos - row_offset, 0, tok_rows - 1) for end_pos in prompt_ends]
        span_logs = lax.all_gather(
            jnp.stack([cum_log[tok_rows - 1], cum_log[local_ends[0]], cum_log[local_ends[1]]]),
            "seq",
        )
        state_rows, end_rows = span_weights(span_logs, lengths, tok_rows, seq_count)
        in_block, carried, increment = block_terms(
            queries, key_rows, values, log_forget, in_gate, segment, seg_before
        )
        parts = [increment] + [
            end_part(
                key_rows,
                values,
                cum_log,
                in_gate,
                segment,
                local_ends[prompt],
                prompt,
                holders[prompt],
            )
            for prompt in range(PROMPTS - 1)
        ]
        slab = head_width // seq_count
        sent = jnp.stack(
            [part.astype(jnp.bfloat16).reshape(seq_count, slab, -1) for part in parts], axis=1
        )
        got = lax.all_to_all(sent, "seq", 0, 0, tiled=True).astype(jnp.float32)
        spans = got[:, 0]
        states = mix_spans(state_rows, spans).astype(jnp.bfloat16)
        state_here = lax.all_to_all(states, "seq", 0, 0, tiled=True).reshape(head_width, -1)
        own_ends = jnp.sum(got[:, 1:], axis=0)
        ends = mix_spans(end_rows, spans) + jnp.concatenate(
            [own_ends, jnp.zeros_like(own_ends[:1])], axis=0
        )
        sent_states.append(lax.all_gather(ends.astype(jnp.bfloat16), "seq", axis=1, tiled=True))
        hidden_parts = in_block + carried[:, None] * jnp.dot(
            queries, state_here, preferred_element_type=jnp.float32
        )
        sums_one, sums_two = lax.psum(
            (jnp.sum(hidden_parts, axis=1), jnp.sum(hidden_parts * hidden_parts, axis=1)), "wc"
        )
        row_mean = sums_one / head_width
        row_var = sums_two / head_width - row_mean * row_mean
        normal_rows = (hidden_parts - row_mean[:, None]) * lax.rsqrt(row_var + EPSILON)[:, None]
        gated = (
            (
                normal_rows * norm_gain[layer_idx]
                + skip_gain[layer_idx] * conv_act.astype(jnp.float32)
            )
            * jax.nn.silu(outgate)
        ).astype(jnp.bfloat16)
        term_rows = jnp.dot(gated, w_down[layer_idx], preferred_element_type=jnp.float32)
        terms = lax.all_to_all(
            term_rows.astype(jnp.bfloat16), ("wr", "wc"), 1, 0, tiled=True
        ).reshape(-1, tok_rows, current.shape[1])
        summed = jnp.sum(terms.astype(jnp.float32), axis=0)
        current = (current.astype(jnp.float32) + summed).astype(jnp.bfloat16)
        for prompt in range(PROMPTS):
            window = lax.dynamic_slice_in_dim(extended, local_ends[prompt] + 1, CONV - 1, 0)
            edge_pos = prompt_ends[prompt] - (CONV - 2) + jnp.arange(CONV - 1, dtype=jnp.int32)
            sent_edges.append(
                jnp.where(
                    ((edge_pos >= prompt_starts[prompt]) & holders[prompt])[:, None],
                    window,
                    jnp.zeros_like(window),
                )
            )
    state_stack = jnp.stack(sent_states)
    edge_stack = lax.psum(jnp.stack(sent_edges), "seq")
    edge_stack = edge_stack.reshape(LAYERS, PROMPTS, edge_stack.shape[1], edge_stack.shape[2])
    chooser = (request_prompt[:, None] == jnp.arange(PROMPTS, dtype=jnp.int32)[None, :]).astype(
        jnp.bfloat16
    )
    request_state = jnp.einsum(
        "rp,lphd->lrhd", chooser, state_stack, preferred_element_type=jnp.float32
    ).astype(jnp.bfloat16)[:, :, None]
    request_conv = jnp.einsum(
        "rp,lpkc->lrkc", chooser, edge_stack, preferred_element_type=jnp.float32
    ).astype(jnp.bfloat16)
    return (current, request_state, request_conv)


def solution(mesh):
    return jax.shard_map(
        body,
        mesh=mesh,
        in_specs=(
            P("seq", ("wr", "wc")),
            P(),
            P(None, None, ("wr", "wc")),
            P(None, None, ("wr", "wc")),
            P(),
            P(),
            P(None, None, ("wr", "wc")),
            P(None, ("wr", "wc")),
            P(None, "wr", None, None, None),
            P(None, "wr", None, None, None),
            P(None, "wr", None, "wc", None),
            P(None, ("wr", "wc")),
            P(None, ("wr", "wc")),
            P(None, ("wr", "wc"), None),
            P(),
            P("seq"),
        ),
        out_specs=(
            P("seq", ("wr", "wc")),
            P(None, "seq", "wr", None, "wc"),
            P(None, "seq", None, ("wr", "wc")),
        ),
        check_vma=False,
    )
```

profile of v0, /device:TPU:16, one launch (start us, length us, event | category | flops | bytes accessed | tf_op | source)
XLA Modules:
  0.0 664.2 jit_solution(5510766327636577990)
XLA Ops:
  14.5 49.2 %all-gather.11.cloned.1.call-done = bf16[512,2048]{1,0:T(8,128)(2,1)} async-done(((bf16[512,128]{1,0:T(8,128)(2,1)}), bf16[512,2048]{1,0:T(8,128)(2,1)}) %all-gather.11.cloned.1.call-update) | async-done | bytes 2097168 | tf_op jit(solution)/shard_map/all_gather | solution.py:153
  83.3 3.7 exponential_select_fusion.7
  86.9 5.6 all-gather.15.cloned.1.call-done
  96.0 21.3 %all-gather.13.cloned.1.call-done = bf16[512,1024]{1,0:T(8,128)(2,1)} async-done(((bf16[512,256]{1,0:T(8,128)(2,1)}), bf16[512,1024]{1,0:T(8,128)(2,1)}) %all-gather.13.cloned.1.call-update) | async-done | bytes 1048592 | tf_op jit(solution)/shard_map/all_gather | solution.py:171
  120.5 3.3 fusion.74
  136.0 7.3 %all-to-all-start = ((bf16[16,3,64,256]{3,2,1,0:T(8,128)(2,1)}), bf16[16,3,64,256]{3,2,1,0:T(8,128)(2,1)}, u32[]{:S(2)}, u32[]{:S(2)}) async-start(bf16[16,3,64,256]{3,2,1,0:T(8,128)(2,1)} %pad_maximum_fusion.6), calls=%async_computation | async-start | bytes 3145728 | tf_op jit(solution)/shard_map/all_to_all | solution.py:209
  149.7 56.5 %all-reduce.2 = f32[48]{0:T(128)S(1)} all-reduce(f32[48]{0:T(128)S(1)} %maximum_dynamic-update-slice_fusion), channel_id=2, replica_groups=mesh['seq'=16,'wr'=4,'wc'=4] {'seq'}, use_global_device_ids=true, to_apply=%add.2 | all-reduce | flops 48 | bytes 384
  213.4 6.7 %all-to-all-start.1 = ((bf16[16,64,256]{2,1,0:T(8,128)(2,1)}), bf16[16,64,256]{2,1,0:T(8,128)(2,1)}, u32[]{:S(2)}, u32[]{:S(2)}) async-start(bf16[16,64,256]{2,1,0:T(8,128)(2,1)} %multiply_reduce_fusion.1), calls=%async_computation.1 | async-start | bytes 1048576 | tf_op jit(solution)/shard_map/all_to_all | solution.py:212
  221.4 3.2 fusion.21
  226.8 3.5 fusion.28
  230.4 3.3 all-to-all-done.1
  236.5 7.1 %all-reduce.5 = (f32[512]{0:T(512)S(1)}, f32[512]{0:T(512)S(1)}) all-reduce(f32[512]{0:T(512)S(1)} %get-tuple-element.28, f32[512]{0:T(512)S(1)} %get-tuple-element.27), channel_id=1, replica_groups=mesh['seq'=16,'wr'=4,'wc'=4] {'wc'}, use_global_device_ids=true, to_apply=%region_11.12 | all-reduce | flops 1024 | bytes 8192 | tf_op jit(solution)/shard_map/psum | solution.py:221
  243.6 6.0 fusion.17
  251.8 32.7 %all_to_all.46 = bf16[512,16,128]{2,0,1:T(8,128)(2,1)S(1)} all-to-all(bf16[512,16,128]{2,0,1:T(8,128)(2,1)S(1)} %bitcast.288), channel_id=1, replica_groups=mesh['seq'=16,'wr'=4,'wc'=4] {'wr','wc'}, dimensions={1} | all-to-all | bytes 4194304 | tf_op jit(solution)/shard_map/all_to_all | solution.py:235
  286.4 46.1 %all-gather.17.cloned.1.call-done = bf16[512,2048]{1,0:T(8,128)(2,1)} async-done(((bf16[512,128]{1,0:T(8,128)(2,1)}), bf16[512,2048]{1,0:T(8,128)(2,1)}) %all-gather.17.cloned.1.call-update) | async-done | bytes 2097168 | tf_op jit(solution)/shard_map/all_gather | solution.py:153
  353.7 8.2 %all-gather.21.cloned.1.call-done = bf16[512,1024]{1,0:T(8,128)(2,1)} async-done(((bf16[512,256]{1,0:T(8,128)(2,1)}), bf16[512,1024]{1,0:T(8,128)(2,1)}) %all-gather.21.cloned.1.call-update) | async-done | bytes 1048592 | tf_op jit(solution)/shard_map/all_gather | solution.py:170
  364.5 3.4 multiply_reduce_fusion.4
  369.0 17.5 %all-gather.19.cloned.1.call-done = bf16[512,1024]{1,0:T(8,128)(2,1)} async-done(((bf16[512,256]{1,0:T(8,128)(2,1)}), bf16[512,1024]{1,0:T(8,128)(2,1)}) %all-gather.19.cloned.1.call-update) | async-done | bytes 1048592 | tf_op jit(solution)/shard_map/all_gather | solution.py:171
  389.1 3.8 copy.199
  392.9 4.5 fusion.71
  421.6 7.3 %all-to-all-start.3 = ((bf16[16,3,64,256]{3,2,1,0:T(8,128)(2,1)}), bf16[16,3,64,256]{3,2,1,0:T(8,128)(2,1)}, u32[]{:S(2)}, u32[]{:S(2)}) async-start(bf16[16,3,64,256]{3,2,1,0:T(8,128)(2,1)} %pad_maximum_fusion.7), calls=%async_computation.3 | async-start | bytes 3145728 | tf_op jit(solution)/shard_map/all_to_all | solution.py:209
  433.7 58.0 %all-reduce.3 = f32[48]{0:T(128)S(1)} all-reduce(f32[48]{0:T(128)S(1)} %maximum_dynamic-update-slice_fusion.1), channel_id=3, replica_groups=mesh['seq'=16,'wr'=4,'wc'=4] {'seq'}, use_global_device_ids=true, to_apply=%add.3 | all-reduce | flops 48 | bytes 384
  509.2 6.8 %all-to-all-start.4 = ((bf16[16,64,256]{2,1,0:T(8,128)(2,1)}), bf16[16,64,256]{2,1,0:T(8,128)(2,1)}, u32[]{:S(2)}, u32[]{:S(2)}) async-start(bf16[16,64,256]{2,1,0:T(8,128)(2,1)} %multiply_reduce_fusion), calls=%async_computation.4 | async-start | bytes 1048576 | tf_op jit(solution)/shard_map/all_to_all | solution.py:212
  516.0 3.2 fusion.22
  521.5 3.6 fusion.27
  527.5 4.4 all-to-all-done.4
  534.0 7.2 %all-reduce.4 = (f32[512]{0:T(512)S(1)}, f32[512]{0:T(512)S(1)}) all-reduce(f32[512]{0:T(512)S(1)} %get-tuple-element.26, f32[512]{0:T(512)S(1)} %get-tuple-element.25), channel_id=1, replica_groups=mesh['seq'=16,'wr'=4,'wc'=4] {'wc'}, use_global_device_ids=true, to_apply=%region_24.25 | all-reduce | flops 1024 | bytes 8192 | tf_op jit(solution)/shard_map/psum | solution.py:221
  541.3 5.2 fusion.18
  546.5 3.5 copy.268
  550.0 7.6 %all-to-all-start.5 = ((bf16[512,16,128]{2,0,1:T(8,128)(2,1)}), bf16[512,16,128]{2,0,1:T(8,128)(2,1)S(1)}, u32[]{:S(2)}, u32[]{:S(2)}) async-start(bf16[512,16,128]{2,0,1:T(8,128)(2,1)} %bitcast.287), calls=%async_computation.5 | async-start | bytes 4194304 | tf_op jit(solution)/shard_map/all_to_all | solution.py:235
  559.4 84.2 %psum.39 = bf16[2,3,3,256]{3,1,2,0:T(4,128)(2,1)S(1)} all-reduce(bf16[2,3,3,256]{3,1,2,0:T(4,128)(2,1)S(1)} %copy.221), channel_id=1, replica_groups=mesh['seq'=16,'wr'=4,'wc'=4] {'seq'}, use_global_device_ids=true, to_apply=%region_38.39 | all-reduce | flops 4608 | bytes 18432 | tf_op jit(solution)/shard_map/psum | solution.py:251
  644.5 4.1 copy.271
  (322 shorter events, 155.5 us)
Async XLA Ops:
  7.2 56.5 %all-gather.11.cloned.1.call-start = ((), (), s32[]{:S(2)}) async-start(), calls=%async_computation.6 | async-start | bytes 2228224 | tf_op jit(solution)/shard_map/all_gather | solution.py:153
  7.9 84.7 %all-gather.15.cloned.1.call-start = ((), (), s32[]{:S(2)}) async-start(), calls=%async_computation.8 | async-start | bytes 1310720 | tf_op jit(solution)/shard_map/all_gather | solution.py:170
  12.5 63.7 %copy-start.36 = (s32[512]{0:T(512)}, s32[512]{0:T(512)S(1)}, u32[]{:S(2)}) copy-start(s32[512]{0:T(512)S(1)} %convert_add_fusion) | copy-start | bytes 6148
  67.8 12.2 %copy-start.5 = (bf16[512,2048]{1,0:T(8,128)(2,1)}, bf16[512,2048]{1,0:T(8,128)(2,1)S(1)}, u32[]{:S(2)}) copy-start(bf16[512,2048]{1,0:T(8,128)(2,1)S(1)} %fusion.2) | copy-start | bytes 6291460
  69.2 48.1 %all-gather.13.cloned.1.call-start = ((), (), s32[]{:S(2)}) async-start(), calls=%async_computation.7 | async-start | bytes 1310720 | tf_op jit(solution)/shard_map/all_gather | solution.py:171
  72.5 5.3 collective-permute-start
  80.0 14.5 %copy-start.54 = (f32[4]{0:T(128)}, f32[4]{0:T(128)S(1)}, u32[]{:S(2)}) copy-start(f32[4]{0:T(128)S(1)} %compare_convert_fusion.6) | copy-start | bytes 52
  136.0 71.3 %all-to-all-start = ((bf16[16,3,64,256]{3,2,1,0:T(8,128)(2,1)}), bf16[16,3,64,256]{3,2,1,0:T(8,128)(2,1)}, u32[]{:S(2)}, u32[]{:S(2)}) async-start(bf16[16,3,64,256]{3,2,1,0:T(8,128)(2,1)} %pad_maximum_fusion.6), calls=%async_computation | async-start | bytes 3145728 | tf_op jit(solution)/shard_map/all_to_all | solution.py:209
  146.9 60.4 %copy-start.50 = (s32[17]{0:T(128)}, s32[17]{0:T(128)S(1)}, u32[]{:S(2)}) copy-start(s32[17]{0:T(128)S(1)} %fusion.170) | copy-start | bytes 208
  147.6 59.7 %copy-start.52 = (s32[16]{0:T(128)}, s32[16]{0:T(128)S(1)}, u32[]{:S(2)}) copy-start(s32[16]{0:T(128)S(1)} %fusion.169) | copy-start | bytes 196
  147.6 59.5 %copy-start.31 = (pred[17,16]{0,1:T(8,128)(4,1)}, pred[17,16]{0,1:T(8,128)(4,1)S(1)}, u32[]{:S(2)}) copy-start(pred[17,16]{0,1:T(8,128)(4,1)S(1)} %iota_compare_fusion.2) | copy-start | bytes 820
  147.6 59.5 %copy-start.32 = (pred[16,16]{1,0:T(8,128)(4,1)}, pred[16,16]{1,0:T(8,128)(4,1)S(1)}, u32[]{:S(2)}) copy-start(pred[16,16]{1,0:T(8,128)(4,1)S(1)} %iota_compare_fusion.1) | copy-start | bytes 772
  209.2 11.7 %copy-start.61 = (f32[2,256]{1,0:T(2,128)S(1)}, f32[2,256]{1,0:T(2,128)}, u32[]{:S(2)}) copy-start(f32[2,256]{1,0:T(2,128)} %param.28) | copy-start | bytes 6148
  213.4 20.2 %all-to-all-start.1 = ((bf16[16,64,256]{2,1,0:T(8,128)(2,1)}), bf16[16,64,256]{2,1,0:T(8,128)(2,1)}, u32[]{:S(2)}, u32[]{:S(2)}) async-start(bf16[16,64,256]{2,1,0:T(8,128)(2,1)} %multiply_reduce_fusion.1), calls=%async_computation.1 | async-start | bytes 1048576 | tf_op jit(solution)/shard_map/all_to_all | solution.py:212
  220.2 112.3 %all-gather.17.cloned.1.call-start = ((), (), s32[]{:S(2)}) async-start(), calls=%async_computation.9 | async-start | bytes 2228224 | tf_op jit(solution)/shard_map/all_gather | solution.py:153
  230.4 13.3 %copy-start.20 = (bf16[512,256]{1,0:T(8,128)(2,1)S(1)}, bf16[512,256]{1,0:T(8,128)(2,1)}, u32[]{:S(2)}) copy-start(bf16[512,256]{1,0:T(8,128)(2,1)} %multiply_convert_fusion.5) | copy-start | bytes 786436
  286.1 75.8 %all-gather.21.cloned.1.call-start = ((), (), s32[]{:S(2)}) async-start(), calls=%async_computation.11 | async-start | bytes 1310720 | tf_op jit(solution)/shard_map/all_gather | solution.py:170
  338.5 47.9 %all-gather.19.cloned.1.call-start = ((), (), s32[]{:S(2)}) async-start(), calls=%async_computation.10 | async-start | bytes 1310720 | tf_op jit(solution)/shard_map/all_gather | solution.py:171
  339.2 3.8 collective-permute-start.1
  350.6 38.5 %copy-start.34 = (f32[512]{0:T(512)}, f32[512]{0:T(512)S(1)}, u32[]{:S(2)}) copy-start(f32[512]{0:T(512)S(1)} %get-tuple-element.54) | copy-start | bytes 6148
  421.6 81.6 %all-to-all-start.3 = ((bf16[16,3,64,256]{3,2,1,0:T(8,128)(2,1)}), bf16[16,3,64,256]{3,2,1,0:T(8,128)(2,1)}, u32[]{:S(2)}, u32[]{:S(2)}) async-start(bf16[16,3,64,256]{3,2,1,0:T(8,128)(2,1)} %pad_maximum_fusion.7), calls=%async_computation.3 | async-start | bytes 3145728 | tf_op jit(solution)/shard_map/all_to_all | solution.py:209
  428.9 215.6 %all-gather.23.cloned.1.call-start = ((), (), s32[]{:S(2)}) async-start(), calls=%async_computation.12 | async-start | bytes 1671168 | tf_op jit(solution)/shard_map/all_gather | solution.py:217
  431.7 69.2 %copy-start.51 = (s32[17]{0:T(128)S(1)}, s32[17]{0:T(128)}, u32[]{:S(2)}) copy-start(s32[17]{0:T(128)} %copy-done.50) | copy-start | bytes 208
  431.7 69.2 %copy-start.53 = (s32[16]{0:T(128)S(1)}, s32[16]{0:T(128)}, u32[]{:S(2)}) copy-start(s32[16]{0:T(128)} %copy-done.52) | copy-start | bytes 196
  509.2 22.7 %all-to-all-start.4 = ((bf16[16,64,256]{2,1,0:T(8,128)(2,1)}), bf16[16,64,256]{2,1,0:T(8,128)(2,1)}, u32[]{:S(2)}, u32[]{:S(2)}) async-start(bf16[16,64,256]{2,1,0:T(8,128)(2,1)} %multiply_reduce_fusion), calls=%async_computation.4 | async-start | bytes 1048576 | tf_op jit(solution)/shard_map/all_to_all | solution.py:212
  516.0 134.2 %all-gather.25.cloned.1.call-start = ((), (), s32[]{:S(2)}) async-start(), calls=%async_computation.13 | async-start | bytes 1671168 | tf_op jit(solution)/shard_map/all_gather | solution.py:217
  526.8 14.5 %copy-start.4 = (bf16[512,2048]{1,0:T(8,128)(2,1)S(1)}, bf16[512,2048]{1,0:T(8,128)(2,1)}, u32[]{:S(2)}) copy-start(bf16[512,2048]{1,0:T(8,128)(2,1)} %copy-done.3) | copy-start | bytes 6291460
  526.8 14.5 %copy-start.19 = (bf16[512,256]{1,0:T(8,128)(2,1)S(1)}, bf16[512,256]{1,0:T(8,128)(2,1)}, u32[]{:S(2)}) copy-start(bf16[512,256]{1,0:T(8,128)(2,1)} %multiply_convert_fusion.3) | copy-start | bytes 786436
  526.8 14.5 %copy-start.66 = (f32[1,256]{1,0:T(1,128)S(1)}, f32[1,256]{1,0:T(1,128)}, u32[]{:S(2)}) copy-start(f32[1,256]{1,0:T(1,128)} %get-tuple-element.102) | copy-start | bytes 3076
  526.8 14.5 %copy-start.67 = (f32[1,256]{1,0:T(1,128)S(1)}, f32[1,256]{1,0:T(1,128)}, u32[]{:S(2)}) copy-start(f32[1,256]{1,0:T(1,128)} %get-tuple-element.100) | copy-start | bytes 3076
  550.0 93.7 %copy-start.70 = (s32[2]{0:T(128)S(1)}, s32[2]{0:T(128)}, u32[]{:S(2)}) copy-start(s32[2]{0:T(128)} %param.31) | copy-start | bytes 28
  550.0 98.6 %all-to-all-start.5 = ((bf16[512,16,128]{2,0,1:T(8,128)(2,1)}), bf16[512,16,128]{2,0,1:T(8,128)(2,1)S(1)}, u32[]{:S(2)}, u32[]{:S(2)}) async-start(bf16[512,16,128]{2,0,1:T(8,128)(2,1)} %bitcast.287), calls=%async_computation.5 | async-start | bytes 4194304 | tf_op jit(solution)/shard_map/all_to_all | solution.py:235
  (55 other events, 284.2 us)
Sparse Core Ops, SparseCore 0:
  10.6 53.0 all-gather.10
  69.3 23.1 all-gather.14
  94.4 22.8 all-gather.12
  286.2 46.2 all-gather.16
  338.6 23.1 all-gather.20
  363.5 22.8 all-gather.18
  499.2 73.1 all-gather.22
  574.1 70.0 all-gather.24
where the time goes:
time: 669 us; the launch traced here: 664 us
  blocking collectives  246 us (37%)
  waiting for transfers between devices  158 us (24%)
  local copies, waits for them, and re-layouts  72 us (11%)
  other arithmetic  69.9 us (10%)
  matrix products  56.6 us (8%)
  starting transfers between devices  41.7 us (6%)
  between operations  20.6 us (3%)
    unnamed x2, blocking collectives  114 us
    all_gather x2, waiting for transfers between devices, body(): gathered = lax.all_gather(current, ('wr', 'wc'), axis=1, tiled=True)  95.3 us
    psum x1, blocking collectives, body(): edge_stack = lax.psum(jnp.stack(sent_edges), 'seq')  84.2 us
    all_gather x2, waiting for transfers between devices, body(): lax.all_gather(conv_act, 'wc', axis=1, tiled=True)  38.8 us
    all_to_all x1, blocking collectives, body(): lax.all_to_all(term_rows.astype(jnp.bfloat16), ('wr', 'wc'), 1, 0, tiled=...  32.7 us
    unnamed x154, local copies, waits for them, and re-layouts  15 us
    all_to_all x2, starting transfers between devices, body(): got = lax.all_to_all(sent, 'seq', 0, 0, tiled=True).astype(jnp.float32)  14.6 us
    psum x2, blocking collectives, body(): lax.psum((jnp.sum(hidden_parts, axis=1), jnp.sum(hidden_parts * hidden_pa...  14.3 us
  transfers between devices with their start and end apart: 15, of which 9 were waited for; matrix products, arithmetic and copies ran while one was open for 16% of the time, Pallas kernels for 0%

commit v1 on v0

--- a/solution.py
+++ b/solution.py
@@ -232,8 +232,16 @@
             * jax.nn.silu(outgate)
         ).astype(jnp.bfloat16)
         term_rows = jnp.dot(gated, w_down[layer_idx], preferred_element_type=jnp.float32)
-        terms = lax.all_to_all(
-            term_rows.astype(jnp.bfloat16), ("wr", "wc"), 1, 0, tiled=True
+        terms = jnp.concatenate(
+            lax.all_to_all(
+                jnp.stack(
+                    jnp.split(term_rows.astype(jnp.bfloat16), lax.axis_size(("wr", "wc")), axis=1)
+                ),
+                ("wr", "wc"),
+                0,
+                0,
+            ),
+            axis=0,
         ).reshape(-1, tok_rows, current.shape[1])
         summed = jnp.sum(terms.astype(jnp.float32), axis=0)
         current = (current.astype(jnp.float32) + summed).astype(jnp.bfloat16)

time: 669 us -> 726 us (1.085); the launches traced: 664 us -> 714 us
  local copies, waits for them, and re-layouts: 72 us -> 107 us
  blocking collectives: 246 us -> 263 us
    unnamed x154 -> x168, local copies, waits for them, and re-layouts: 15 us -> 51.5 us
    psum x1, blocking collectives: 84.2 us -> 100 us  [body(): edge_stack = lax.psum(jnp.stack(sent_edges), 'seq')]
  transfers between devices with their start and end apart: 15 -> 15, of which waited for: 9 -> 8; matrix products, arithmetic and copies ran while one was open for 16% -> 19% of each run, Pallas kernels for 0% -> 0%
where the time goes in v1:
time: 726 us; the launch traced here: 714 us
  blocking collectives  263 us (36%)
  waiting for transfers between devices  155 us (21%)
  local copies, waits for them, and re-layouts  107 us (15%)
  other arithmetic  72.6 us (10%)
  matrix products  56.6 us (8%)
  starting transfers between devices  38.8 us (5%)
  between operations  21 us (3%)
    unnamed x2, blocking collectives  115 us
    psum x1, blocking collectives, body(): edge_stack = lax.psum(jnp.stack(sent_edges), 'seq')  100 us
    all_gather x2, waiting for transfers between devices, body(): gathered = lax.all_gather(current, ('wr', 'wc'), axis=1, tiled=True)  96.5 us
    unnamed x168, local copies, waits for them, and re-layouts  51.5 us
    all_gather x2, waiting for transfers between devices, body(): lax.all_gather(conv_act, 'wc', axis=1, tiled=True)  38.8 us
    all_to_all x1, blocking collectives, body(): lax.all_to_all(jnp.stack(jnp.split(term_rows.astype(jnp.bfloat16), lax.ax...  32.7 us
    psum x2, blocking collectives, body(): lax.psum((jnp.sum(hidden_parts, axis=1), jnp.sum(hidden_parts * hidden_pa...  15.3 us
    all_to_all x2, starting transfers between devices, body(): got = lax.all_to_all(sent, 'seq', 0, 0, tiled=True).astype(jnp.float32)  14.6 us
  transfers between devices with their start and end apart: 15, of which 8 were waited for; matrix products, arithmetic and copies ran while one was open for 19% of the time, Pallas kernels for 0%

profile of v1, /device:TPU:16, one launch (start us, length us, event | category | flops | bytes accessed | tf_op | source)
XLA Modules:
  0.0 713.7 jit_solution(2202268877119423511)
XLA Ops:
  14.8 48.9 %all-gather.11.cloned.1.call-done = bf16[512,2048]{1,0:T(8,128)(2,1)} async-done(((bf16[512,128]{1,0:T(8,128)(2,1)}), bf16[512,2048]{1,0:T(8,128)(2,1)}) %all-gather.11.cloned.1.call-update) | async-done | bytes 2097168 | tf_op jit(solution)/shard_map/all_gather | solution.py:153
  83.0 3.8 exponential_select_fusion.7
  86.8 5.8 all-gather.15.cloned.1.call-done
  96.0 21.3 %all-gather.13.cloned.1.call-done = bf16[512,1024]{1,0:T(8,128)(2,1)} async-done(((bf16[512,256]{1,0:T(8,128)(2,1)}), bf16[512,1024]{1,0:T(8,128)(2,1)}) %all-gather.13.cloned.1.call-update) | async-done | bytes 1048592 | tf_op jit(solution)/shard_map/all_gather | solution.py:171
  120.6 3.3 fusion.72
  136.1 7.3 %all-to-all-start = ((bf16[16,3,64,256]{3,2,1,0:T(8,128)(2,1)}), bf16[16,3,64,256]{3,2,1,0:T(8,128)(2,1)}, u32[]{:S(2)}, u32[]{:S(2)}) async-start(bf16[16,3,64,256]{3,2,1,0:T(8,128)(2,1)} %pad_maximum_fusion.6), calls=%async_computation | async-start | bytes 3145728 | tf_op jit(solution)/shard_map/all_to_all | solution.py:209
  149.4 56.8 %all-reduce.2 = f32[48]{0:T(128)S(1)} all-reduce(f32[48]{0:T(128)S(1)} %maximum_dynamic-update-slice_fusion), channel_id=2, replica_groups=mesh['seq'=16,'wr'=4,'wc'=4] {'seq'}, use_global_device_ids=true, to_apply=%add.2 | all-reduce | flops 48 | bytes 384
  210.3 3.2 multiply_reduce_fusion.1
  213.5 6.7 all-to-all-start.1
  223.0 3.2 fusion.19
  228.4 3.5 fusion.26
  236.5 7.7 %all-reduce.5 = (f32[512]{0:T(512)S(1)}, f32[512]{0:T(512)}) all-reduce(f32[512]{0:T(512)S(1)} %get-tuple-element.28, f32[512]{0:T(512)S(1)} %get-tuple-element.27), channel_id=1, replica_groups=mesh['seq'=16,'wr'=4,'wc'=4] {'wc'}, use_global_device_ids=true, to_apply=%region_11.12 | all-reduce | flops 1024 | bytes 8192 | tf_op jit(solution)/shard_map/psum | solution.py:221
  244.9 6.0 convolution_convert_fusion.1
  265.8 32.7 %all_to_all.30 = bf16[16,512,128]{2,1,0:T(8,128)(2,1)S(1)} all-to-all(bf16[16,512,128]{2,1,0:T(8,128)(2,1)S(1)} %fusion.145), channel_id=1, replica_groups=mesh['seq'=16,'wr'=4,'wc'=4] {'wr','wc'}, dimensions={0} | all-to-all | bytes 4194304 | tf_op jit(solution)/shard_map/all_to_all | solution.py:236
  300.4 47.7 %all-gather.17.cloned.1.call-done = bf16[512,2048]{1,0:T(8,128)(2,1)} async-done(((bf16[512,128]{1,0:T(8,128)(2,1)}), bf16[512,2048]{1,0:T(8,128)(2,1)}) %all-gather.17.cloned.1.call-update) | async-done | bytes 2097168 | tf_op jit(solution)/shard_map/all_gather | solution.py:153
  371.1 6.3 all-gather.21.cloned.1.call-done
  380.1 3.3 multiply_reduce_fusion.4
  384.5 17.5 %all-gather.19.cloned.1.call-done = bf16[512,1024]{1,0:T(8,128)(2,1)} async-done(((bf16[512,256]{1,0:T(8,128)(2,1)}), bf16[512,1024]{1,0:T(8,128)(2,1)}) %all-gather.19.cloned.1.call-update) | async-done | bytes 1048592 | tf_op jit(solution)/shard_map/all_gather | solution.py:171
  404.6 3.8 copy.192
  408.5 4.5 fusion.69
  415.9 3.2 fusion.14
  437.0 7.3 %all-to-all-start.3 = ((bf16[16,3,64,256]{3,2,1,0:T(8,128)(2,1)}), bf16[16,3,64,256]{3,2,1,0:T(8,128)(2,1)}, u32[]{:S(2)}, u32[]{:S(2)}) async-start(bf16[16,3,64,256]{3,2,1,0:T(8,128)(2,1)} %pad_maximum_fusion.7), calls=%async_computation.3 | async-start | bytes 3145728 | tf_op jit(solution)/shard_map/all_to_all | solution.py:209
  449.4 57.7 %all-reduce.3 = f32[48]{0:T(128)S(1)} all-reduce(f32[48]{0:T(128)S(1)} %maximum_dynamic-update-slice_fusion.1), channel_id=3, replica_groups=mesh['seq'=16,'wr'=4,'wc'=4] {'seq'}, use_global_device_ids=true, to_apply=%add.3 | all-reduce | flops 48 | bytes 384
  523.7 6.7 all-to-all-start.4
  530.5 3.2 fusion.20
  536.0 3.6 fusion.25
  542.0 5.0 all-to-all-done.4
  549.2 7.6 %all-reduce.4 = (f32[512]{0:T(512)S(1)}, f32[512]{0:T(512)S(1)}) all-reduce(f32[512]{0:T(512)S(1)} %get-tuple-element.26, f32[512]{0:T(512)S(1)} %get-tuple-element.25), channel_id=1, replica_groups=mesh['seq'=16,'wr'=4,'wc'=4] {'wc'}, use_global_device_ids=true, to_apply=%region_24.25 | all-reduce | flops 1024 | bytes 8192 | tf_op jit(solution)/shard_map/psum | solution.py:221
  556.8 5.2 convolution_convert_fusion
  587.0 5.2 all-to-all-start.5
  592.7 100.3 %psum.39 = bf16[2,3,3,256]{3,1,2,0:T(4,128)(2,1)S(1)} all-reduce(bf16[2,3,3,256]{3,1,2,0:T(4,128)(2,1)S(1)} %copy.213), channel_id=1, replica_groups=mesh['seq'=16,'wr'=4,'wc'=4] {'seq'}, use_global_device_ids=true, to_apply=%region_38.39 | all-reduce | flops 4608 | bytes 18432 | tf_op jit(solution)/shard_map/psum | solution.py:259
  693.9 4.1 copy.257
  (336 shorter events, 190.1 us)
Async XLA Ops:
  7.2 56.5 %all-gather.11.cloned.1.call-start = ((), (), s32[]{:S(2)}) async-start(), calls=%async_computation.6 | async-start | bytes 2228224 | tf_op jit(solution)/shard_map/all_gather | solution.py:153
  7.9 84.7 %all-gather.15.cloned.1.call-start = ((), (), s32[]{:S(2)}) async-start(), calls=%async_computation.8 | async-start | bytes 1310720 | tf_op jit(solution)/shard_map/all_gather | solution.py:170
  12.7 63.1 %copy-start.32 = (s32[512]{0:T(512)}, s32[512]{0:T(512)S(1)}, u32[]{:S(2)}) copy-start(s32[512]{0:T(512)S(1)} %convert_add_fusion) | copy-start | bytes 6148
  67.8 11.9 %copy-start.5 = (bf16[512,2048]{1,0:T(8,128)(2,1)}, bf16[512,2048]{1,0:T(8,128)(2,1)S(1)}, u32[]{:S(2)}) copy-start(bf16[512,2048]{1,0:T(8,128)(2,1)S(1)} %fusion.2) | copy-start | bytes 6291460
  69.2 10.4 %copy-start.22 = (bf16[2,2048,8]{1,2,0:T(8,128)(2,1)S(1)}, bf16[2,2048,8]{1,2,0:T(8,128)(2,1)}, u32[]{:S(2)}) copy-start(bf16[2,2048,8]{1,2,0:T(8,128)(2,1)} %param.20) | copy-start | bytes 196612
  69.3 48.1 %all-gather.13.cloned.1.call-start = ((), (), s32[]{:S(2)}) async-start(), calls=%async_computation.7 | async-start | bytes 1310720 | tf_op jit(solution)/shard_map/all_gather | solution.py:171
  70.7 9.6 %copy-start.25 = (f32[512]{0:T(512)}, f32[512]{0:T(512)S(1)}, u32[]{:S(2)}) copy-start(f32[512]{0:T(512)S(1)} %get-tuple-element.97) | copy-start | bytes 6148
  72.6 4.8 collective-permute-start
  136.1 71.3 %all-to-all-start = ((bf16[16,3,64,256]{3,2,1,0:T(8,128)(2,1)}), bf16[16,3,64,256]{3,2,1,0:T(8,128)(2,1)}, u32[]{:S(2)}, u32[]{:S(2)}) async-start(bf16[16,3,64,256]{3,2,1,0:T(8,128)(2,1)} %pad_maximum_fusion.6), calls=%async_computation | async-start | bytes 3145728 | tf_op jit(solution)/shard_map/all_to_all | solution.py:209
  146.5 60.8 %copy-start.47 = (s32[17]{0:T(128)}, s32[17]{0:T(128)S(1)}, u32[]{:S(2)}) copy-start(s32[17]{0:T(128)S(1)} %fusion.200) | copy-start | bytes 208
  147.3 60.1 %copy-start.48 = (s32[16]{0:T(128)}, s32[16]{0:T(128)S(1)}, u32[]{:S(2)}) copy-start(s32[16]{0:T(128)S(1)} %fusion.199) | copy-start | bytes 196
  147.3 59.8 %copy-start.27 = (pred[17,16]{0,1:T(8,128)(4,1)}, pred[17,16]{0,1:T(8,128)(4,1)S(1)}, u32[]{:S(2)}) copy-start(pred[17,16]{0,1:T(8,128)(4,1)S(1)} %iota_compare_fusion.2) | copy-start | bytes 820
  147.3 59.8 %copy-start.28 = (pred[16,16]{1,0:T(8,128)(4,1)}, pred[16,16]{1,0:T(8,128)(4,1)S(1)}, u32[]{:S(2)}) copy-start(pred[16,16]{1,0:T(8,128)(4,1)S(1)} %iota_compare_fusion.1) | copy-start | bytes 772
  213.5 20.2 %all-to-all-start.1 = ((bf16[16,64,256]{2,1,0:T(8,128)(2,1)}), bf16[16,64,256]{2,1,0:T(8,128)(2,1)}, u32[]{:S(2)}, u32[]{:S(2)}) async-start(bf16[16,64,256]{2,1,0:T(8,128)(2,1)} %multiply_reduce_fusion.1), calls=%async_computation.1 | async-start | bytes 1048576 | tf_op jit(solution)/shard_map/all_to_all | solution.py:212
  220.2 127.8 %all-gather.17.cloned.1.call-start = ((), (), s32[]{:S(2)}) async-start(), calls=%async_computation.9 | async-start | bytes 2228224 | tf_op jit(solution)/shard_map/all_gather | solution.py:153
  231.9 13.0 %copy-start.20 = (bf16[512,256]{1,0:T(8,128)(2,1)S(1)}, bf16[512,256]{1,0:T(8,128)(2,1)}, u32[]{:S(2)}) copy-start(bf16[512,256]{1,0:T(8,128)(2,1)} %multiply_convert_fusion.5) | copy-start | bytes 786436
  300.1 77.3 %all-gather.21.cloned.1.call-start = ((), (), s32[]{:S(2)}) async-start(), calls=%async_computation.11 | async-start | bytes 1310720 | tf_op jit(solution)/shard_map/all_gather | solution.py:170
  354.1 47.9 %all-gather.19.cloned.1.call-start = ((), (), s32[]{:S(2)}) async-start(), calls=%async_computation.10 | async-start | bytes 1310720 | tf_op jit(solution)/shard_map/all_gather | solution.py:171
  356.2 5.3 collective-permute-start.1
  368.0 36.6 %copy-start.30 = (f32[512]{0:T(512)}, f32[512]{0:T(512)S(1)}, u32[]{:S(2)}) copy-start(f32[512]{0:T(512)S(1)} %get-tuple-element.54) | copy-start | bytes 6148
  437.0 9.2 %copy-start.56 = (f32[16]{0:T(128)S(1)}, f32[16]{0:T(128)}, u32[]{:S(2)}) copy-start(f32[16]{0:T(128)} %get-tuple-element.33) | copy-start | bytes 196
  437.0 9.2 %copy-start.57 = (f32[16]{0:T(128)S(1)}, f32[16]{0:T(128)}, u32[]{:S(2)}) copy-start(f32[16]{0:T(128)} %get-tuple-element.34) | copy-start | bytes 196
  437.0 80.6 %all-to-all-start.3 = ((bf16[16,3,64,256]{3,2,1,0:T(8,128)(2,1)}), bf16[16,3,64,256]{3,2,1,0:T(8,128)(2,1)}, u32[]{:S(2)}, u32[]{:S(2)}) async-start(bf16[16,3,64,256]{3,2,1,0:T(8,128)(2,1)} %pad_maximum_fusion.7), calls=%async_computation.3 | async-start | bytes 3145728 | tf_op jit(solution)/shard_map/all_to_all | solution.py:209
  444.3 249.5 %all-gather.23.cloned.1.call-start = ((), (), s32[]{:S(2)}) async-start(), calls=%async_computation.12 | async-start | bytes 1671168 | tf_op jit(solution)/shard_map/all_gather | solution.py:217
  523.7 23.3 %all-to-all-start.4 = ((bf16[16,64,256]{2,1,0:T(8,128)(2,1)}), bf16[16,64,256]{2,1,0:T(8,128)(2,1)}, u32[]{:S(2)}, u32[]{:S(2)}) async-start(bf16[16,64,256]{2,1,0:T(8,128)(2,1)} %multiply_reduce_fusion), calls=%async_computation.4 | async-start | bytes 1048576 | tf_op jit(solution)/shard_map/all_to_all | solution.py:212
  530.5 167.5 %all-gather.25.cloned.1.call-start = ((), (), s32[]{:S(2)}) async-start(), calls=%async_computation.13 | async-start | bytes 1671168 | tf_op jit(solution)/shard_map/all_gather | solution.py:217
  541.2 15.5 %copy-start.4 = (bf16[512,2048]{1,0:T(8,128)(2,1)S(1)}, bf16[512,2048]{1,0:T(8,128)(2,1)}, u32[]{:S(2)}) copy-start(bf16[512,2048]{1,0:T(8,128)(2,1)} %copy-done.3) | copy-start | bytes 6291460
  541.3 15.5 %copy-start.19 = (bf16[512,256]{1,0:T(8,128)(2,1)S(1)}, bf16[512,256]{1,0:T(8,128)(2,1)}, u32[]{:S(2)}) copy-start(bf16[512,256]{1,0:T(8,128)(2,1)} %multiply_convert_fusion.3) | copy-start | bytes 786436
  541.3 15.5 %copy-start.58 = (f32[1,256]{1,0:T(1,128)S(1)}, f32[1,256]{1,0:T(1,128)}, u32[]{:S(2)}) copy-start(f32[1,256]{1,0:T(1,128)} %get-tuple-element.102) | copy-start | bytes 3076
  541.3 15.5 %copy-start.59 = (f32[1,256]{1,0:T(1,128)S(1)}, f32[1,256]{1,0:T(1,128)}, u32[]{:S(2)}) copy-start(f32[1,256]{1,0:T(1,128)} %get-tuple-element.100) | copy-start | bytes 3076
  587.0 106.0 %copy-start.62 = (s32[2]{0:T(128)S(1)}, s32[2]{0:T(128)}, u32[]{:S(2)}) copy-start(s32[2]{0:T(128)} %param.31) | copy-start | bytes 28
  587.0 118.1 %all-to-all-start.5 = ((bf16[16,512,128]{2,1,0:T(8,128)(2,1)}), bf16[16,512,128]{2,1,0:T(8,128)(2,1)S(1)}, u32[]{:S(2)}, u32[]{:S(2)}) async-start(bf16[16,512,128]{2,1,0:T(8,128)(2,1)} %fusion.129), calls=%async_computation.5 | async-start | bytes 4194304 | tf_op jit(solution)/shard_map/all_to_all | solution.py:236
  (47 other events, 200.4 us)
Sparse Core Ops, SparseCore 0:
  10.6 53.0 all-gather.10
  69.4 23.1 all-gather.14
  94.4 22.8 all-gather.12
  300.3 47.7 all-gather.16
  354.2 23.1 all-gather.20
  379.1 22.8 all-gather.18
  514.8 72.4 all-gather.22
  589.1 70.6 all-gather.24
